TPU v7x, 32 devices: a whole 2x2x4 slice. The times are simulated.
32 devices in a mesh: seq: 4 (over y, x), dp: 8 (over z, core).
Axes of the slice: x: 2, y: 2, z: 4, core: 2. Of those that a mesh axis runs over, the one named last changes fastest.
Arguments:
- tokens: bfloat16 [8, 2048, 768], P('dp', 'seq'), may hold values from -6 to 6
- doc_start: int32 [8, 2048], P('dp'), may hold values from 0 to 2047, as said below
- cotangent: bfloat16 [8, 2048, 768], P('dp', 'seq'), may hold values from -6 to 6
- norm_one: float32 [768], replicated, may hold values from 0.5 to 1.5
- w_qkv: bfloat16 [768, 2304], replicated, may hold values from -0.21875 to 0.21875
- w_out: bfloat16 [768, 768], replicated, may hold values from -0.875 to 0.875
- norm_two: float32 [768], replicated, may hold values from 0.5 to 1.5
- w_in: bfloat16 [768, 2304], replicated, may hold values from -0.21875 to 0.21875
- w_down: bfloat16 [1152, 768], replicated, may hold values from -0.1875 to 0.1875
Outputs:
- result: bfloat16 [8, 2048, 768], P('dp', 'seq')
- grad_tokens: float32 [8, 2048, 768], P('dp', 'seq')
- grad_norm_one: float32 [768], replicated
- grad_w_qkv: float32 [768, 2304], replicated
- grad_w_out: float32 [768, 768], replicated
- grad_norm_two: float32 [768], replicated
- grad_w_in: float32 [768, 2304], replicated
- grad_w_down: float32 [1152, 768], replicated
Inputs may be any that keep to these rules, and one draw needn't show every extreme that they name: Documents are contiguous: doc_start of a token is the place of the first token of its run of equal values, which begins at a place equal to that value; every row begins a document at 0 and ends with a document of one token at place 2048 - 1, and in every row one document starts before 2048 / 8 and runs to place 7 * 256 - 1 or further.
All inputs are finite; a program needn't handle non-finite values.
Results may differ from a plain program's by a relative error of at most 0.013.
Values may be sent and summed in bfloat16 or wider, within the bound.
No kernel may reach another device: no remote copies, remote signals or barrier semaphores. Data moves between devices by JAX's collectives and lax.ppermute only.
A program may use at most 128 MiB of HBM per device.

v0:
```python
import jax
import jax.numpy as jnp
from jax import lax
from jax.sharding import PartitionSpec as P

D = 768
HEADS = 12
HEAD_DIM = 64
FF = 1152
EPSILON = 1e-05
ROTARY_BASE = 160000.0
SCORE_SCALE = 0.125
MASKED_SCORE = -1e30


def layer_norm(values, gain_vec):
    average = jnp.mean(values, axis=-1, keepdims=True)
    centered = values - average
    variance = jnp.mean(centered * centered, axis=-1, keepdims=True)
    return centered * lax.rsqrt(variance + EPSILON) * gain_vec


def rotary_tables(offset):
    half_dim = HEAD_DIM // 2
    frequency = ROTARY_BASE ** (-(jnp.arange(half_dim, dtype=jnp.float32) * 2.0 / HEAD_DIM))
    angles = offset[:, None] * frequency[None, :]
    return (jnp.cos(angles)[:, None, :], jnp.sin(angles)[:, None, :])


def rotate(values, cosine, sine_table):
    half_dim = values.shape[-1] // 2
    first_half = values[..., :half_dim]
    second_half = values[..., half_dim:]
    return jnp.concatenate(
        [
            first_half * cosine - second_half * sine_table,
            second_half * cosine + first_half * sine_table,
        ],
        axis=-1,
    )


def unrotate_three(grad_wide, cosine, sine_table):
    negative_sine = -sine_table
    return jnp.stack(
        [
            rotate(grad_wide[:, 0], cosine, negative_sine),
            rotate(grad_wide[:, 1], cosine, negative_sine),
            grad_wide[:, 2],
        ],
        axis=1,
    )


def gelu_gate(gate_part, up_part):
    return jax.nn.gelu(gate_part, approximate=False) * up_part


def block_scores(query_block, key_heads, block_ids, starts):
    scores = (
        jnp.einsum("qhd,khd->hqk", query_block, key_heads, preferred_element_type=jnp.float32)
        * SCORE_SCALE
    )
    allowed = block_ids[:, None] == starts[None, :]
    return jnp.where(allowed[None], scores, MASKED_SCORE)


def attend_forward(queries, key_heads, value_heads, starts, block_rows):
    row_total = queries.shape[0]

    def attend_block(block_index):
        row_begin = block_index * block_rows
        query_block = lax.dynamic_slice_in_dim(queries, row_begin, block_rows)
        block_ids = lax.dynamic_slice_in_dim(starts, row_begin, block_rows)
        scores = block_scores(query_block, key_heads, block_ids, starts)
        row_max = jnp.max(scores, axis=-1, keepdims=True)
        weight = jnp.exp(scores - row_max)
        row_sum = jnp.sum(weight, axis=-1, keepdims=True)
        probs = (weight / row_sum).astype(jnp.bfloat16)
        context = jnp.einsum("hqk,khd->qhd", probs, value_heads, preferred_element_type=jnp.float32)
        return (context, row_max, row_sum)

    context, row_max, row_sum = lax.map(
        attend_block, jnp.arange(row_total // block_rows, dtype=jnp.int32)
    )
    return (context.reshape(queries.shape), row_max, row_sum)


def attend_backward(
    queries, key_heads, value_heads, grad_context, starts, row_max, row_sum, block_rows
):
    row_total = queries.shape[0]

    def back_block(carry, block_index):
        grad_key, grad_value = carry
        row_begin = block_index * block_rows
        query_block = lax.dynamic_slice_in_dim(queries, row_begin, block_rows)
        grad_block = lax.dynamic_slice_in_dim(grad_context, row_begin, block_rows)
        block_ids = lax.dynamic_slice_in_dim(starts, row_begin, block_rows)
        scores = block_scores(query_block, key_heads, block_ids, starts)
        probs = jnp.exp(scores - row_max[block_index]) / row_sum[block_index]
        probs_low = probs.astype(jnp.bfloat16)
        grad_value = grad_value + jnp.einsum(
            "hqk,qhd->khd", probs_low, grad_block, preferred_element_type=jnp.float32
        )
        grad_prob = jnp.einsum(
            "qhd,khd->hqk", grad_block, value_heads, preferred_element_type=jnp.float32
        )
        centre = jnp.sum(grad_prob * probs, axis=-1, keepdims=True)
        grad_scores = (probs * (grad_prob - centre)).astype(jnp.bfloat16)
        grad_query = (
            jnp.einsum("hqk,khd->qhd", grad_scores, key_heads, preferred_element_type=jnp.float32)
            * SCORE_SCALE
        )
        grad_key = (
            grad_key
            + jnp.einsum(
                "hqk,qhd->khd", grad_scores, query_block, preferred_element_type=jnp.float32
            )
            * SCORE_SCALE
        )
        return ((grad_key, grad_value), grad_query)

    zero_heads = jnp.zeros(queries.shape, jnp.float32)
    (grad_key, grad_value), grad_query = lax.scan(
        back_block, (zero_heads, zero_heads), jnp.arange(row_total // block_rows, dtype=jnp.int32)
    )
    return (grad_query.reshape(queries.shape), grad_key, grad_value)


def on_device(tokens, doc_start, cotangent, norm_one, w_qkv, w_out, norm_two, w_in, w_down):
    seq_parts = lax.axis_size("seq")
    shard_len = tokens.shape[1]
    row_total = shard_len * seq_parts
    head_width = D // seq_parts
    group_heads = HEADS // seq_parts
    block_rows = min(512, row_total)
    first_token = lax.axis_index("seq") * shard_len
    hidden = tokens[0].astype(jnp.float32)
    starts = doc_start[0]
    own_starts = lax.dynamic_slice_in_dim(starts, first_token, shard_len)
    offset = (first_token + jnp.arange(shard_len, dtype=jnp.int32) - own_starts).astype(jnp.float32)
    cosine, sine_table = rotary_tables(offset)
    normed_one, norm_one_back = jax.vjp(layer_norm, hidden, norm_one)
    normed_one_low = normed_one.astype(jnp.bfloat16)
    projected = jnp.dot(normed_one_low, w_qkv, preferred_element_type=jnp.float32).reshape(
        shard_len, 3, HEADS, HEAD_DIM
    )
    turned = jnp.stack(
        [
            rotate(projected[:, 0], cosine, sine_table),
            rotate(projected[:, 1], cosine, sine_table),
            projected[:, 2],
        ],
        axis=1,
    ).astype(jnp.bfloat16)
    outgoing = turned.reshape(shard_len, 3, seq_parts, head_width)
    incoming = lax.all_to_all(outgoing, "seq", split_axis=2, concat_axis=0, tiled=True)
    queries = incoming[:, 0, 0].reshape(row_total, group_heads, HEAD_DIM)
    key_heads = incoming[:, 1, 0].reshape(row_total, group_heads, HEAD_DIM)
    value_heads = incoming[:, 2, 0].reshape(row_total, group_heads, HEAD_DIM)
    context, row_max, row_sum = attend_forward(queries, key_heads, value_heads, starts, block_rows)
    context_send = context.astype(jnp.bfloat16).reshape(row_total, 1, head_width)
    context_tok = lax.all_to_all(
        context_send, "seq", split_axis=0, concat_axis=1, tiled=True
    ).reshape(shard_len, D)
    attended = jnp.dot(context_tok, w_out, preferred_element_type=jnp.float32)
    middle = hidden + attended
    normed_two, norm_two_back = jax.vjp(layer_norm, middle, norm_two)
    normed_two_low = normed_two.astype(jnp.bfloat16)
    gate_up = jnp.dot(normed_two_low, w_in, preferred_element_type=jnp.float32)
    inner, gelu_back = jax.vjp(gelu_gate, gate_up[:, :FF], gate_up[:, FF:])
    inner_low = inner.astype(jnp.bfloat16)
    result = (middle + jnp.dot(inner_low, w_down, preferred_element_type=jnp.float32)).astype(
        jnp.bfloat16
    )
    grad_out = cotangent[0]
    grad_w_down = jnp.einsum("tf,td->fd", inner_low, grad_out, preferred_element_type=jnp.float32)
    grad_inner = jnp.einsum("td,fd->tf", grad_out, w_down, preferred_element_type=jnp.float32)
    grad_gate, grad_up = gelu_back(grad_inner)
    grad_gate_up = jnp.concatenate([grad_gate, grad_up], axis=-1).astype(jnp.bfloat16)
    grad_w_in = jnp.einsum(
        "td,tf->df", normed_two_low, grad_gate_up, preferred_element_type=jnp.float32
    )
    grad_normed_two = jnp.einsum(
        "tf,df->td", grad_gate_up, w_in, preferred_element_type=jnp.float32
    )
    grad_middle_part, grad_norm_two = norm_two_back(grad_normed_two)
    grad_middle = grad_out.astype(jnp.float32) + grad_middle_part
    grad_mid_low = grad_middle.astype(jnp.bfloat16)
    grad_w_out = jnp.einsum(
        "td,te->de", context_tok, grad_mid_low, preferred_element_type=jnp.float32
    )
    grad_context_tok = jnp.einsum(
        "te,de->td", grad_mid_low, w_out, preferred_element_type=jnp.float32
    ).astype(jnp.bfloat16)
    grad_context = lax.all_to_all(
        grad_context_tok.reshape(shard_len, seq_parts, head_width),
        "seq",
        split_axis=1,
        concat_axis=0,
        tiled=True,
    )
    grad_context = grad_context.reshape(row_total, group_heads, HEAD_DIM)
    grad_query, grad_key, grad_value = attend_backward(
        queries, key_heads, value_heads, grad_context, starts, row_max, row_sum, block_rows
    )
    grad_heads = jnp.stack([grad_query, grad_key, grad_value], axis=1).astype(jnp.bfloat16)
    grad_tok = lax.all_to_all(
        grad_heads.reshape(row_total, 3, 1, head_width),
        "seq",
        split_axis=0,
        concat_axis=2,
        tiled=True,
    )
    grad_tok = grad_tok.reshape(shard_len, 3, HEADS, HEAD_DIM)
    grad_projected = unrotate_three(grad_tok.astype(jnp.float32), cosine, sine_table)
    grad_projected = grad_projected.astype(jnp.bfloat16).reshape(shard_len, 3 * D)
    grad_normed_one = jnp.einsum(
        "tf,df->td", grad_projected, w_qkv, preferred_element_type=jnp.float32
    )
    grad_hidden_part, grad_norm_one = norm_one_back(grad_normed_one)
    grad_input = grad_middle + grad_hidden_part
    grad_w_qkv = jnp.einsum(
        "td,tf->df", normed_one_low, grad_projected, preferred_element_type=jnp.float32
    )
    summed = lax.psum(
        (grad_norm_one, grad_w_qkv, grad_w_out, grad_norm_two, grad_w_in, grad_w_down),
        ("seq", "dp"),
    )
    return (
        result[None],
        grad_input[None],
        summed[0],
        summed[1],
        summed[2],
        summed[3],
        summed[4],
        summed[5],
    )


def solution(mesh):
    placed = (
        P("dp", "seq", None),
        P("dp", None),
        P("dp", "seq", None),
        P(),
        P(),
        P(),
        P(),
        P(),
        P(),
    )
    return jax.shard_map(
        on_device,
        mesh=mesh,
        in_specs=placed,
        out_specs=(P("dp", "seq", None), P("dp", "seq", None), P(), P(), P(), P(), P(), P()),
        check_vma=False,
    )
```

profile of v0, /device:TPU:0, one launch (start us, length us, event | category | flops | bytes accessed | tf_op | source)
XLA Modules:
  0.0 809.1 jit_solution(15965780885867940108)
XLA Ops:
  35.5 28.5 %all-to-all-done = bf16[512,3,4,192]{0,3,1,2:T(8,128)(2,1)} async-done(((bf16[512,3,4,192]{0,3,1,2:T(8,128)(2,1)}), bf16[512,3,4,192]{0,3,1,2:T(8,128)(2,1)}, u32[]{:S(2)}, u32[]{:S(2)}) %all-to-all-start) | async-done | bytes 2359328 | tf_op jit(solution)/shard_map/all_to_all | solution.py:158
  68.4 99.3 %while.29 = (s32[]{:T(128)}, bf16[4,512,3,64]{1,3,2,0:T(8,128)(2,1)}, f32[4,3,512,1]{2,1,3,0:T(4,128)}, f32[4,3,512,1]{2,1,3,0:T(4,128)}, s32[4]{0:T(128)S(1)}, ...) while((s32[]{:T(128)}, ...), condition=%wide.region_5.6_spmd, body=%wide.region_2.5_spmd.sunk | while | flops 844100608 | bytes 53621036 | solution.py:83
  70.4 8.3 %fusion.119 = (f32[3,512]{1,0:T(4,128)S(1)}, f32[3,512,2048]{2,1,0:T(8,128)}) fusion(pred[512,2048]{1,0:T(8,128)(4,1)S(1)} %broadcast_compare_fusion.4, bf16[2048,3,64]{0,2,1:T(8,128)(2,1)} %get-tuple-element.471, bf16[2048,3,64]{0,2,1:T(8,128)(2,1)} %get-tuple-element.470, s32[]{:T(128)S(6)} %select_n.52), kind=kOutput, calls=%fused_computation.3.clone.1 | convolution fusion | flops 412088832 | bytes 14620676 | tf_op jit(solution)/shard_map/while/body/eval_jaxpr/qhd,khd->hqk/dot_general | solution.py:61
  78.7 6.9 fusion.120
  85.6 6.8 fusion.121
  95.2 8.3 %fusion.119 = (f32[3,512]{1,0:T(4,128)S(1)}, f32[3,512,2048]{2,1,0:T(8,128)}) fusion(pred[512,2048]{1,0:T(8,128)(4,1)S(1)} %broadcast_compare_fusion.4, bf16[2048,3,64]{0,2,1:T(8,128)(2,1)} %get-tuple-element.471, bf16[2048,3,64]{0,2,1:T(8,128)(2,1)} %get-tuple-element.470, s32[]{:T(128)S(6)} %select_n.52), kind=kOutput, calls=%fused_computation.3.clone.1 | convolution fusion | flops 412088832 | bytes 14620676 | tf_op jit(solution)/shard_map/while/body/eval_jaxpr/qhd,khd->hqk/dot_general | solution.py:61
  103.5 6.9 fusion.120
  110.4 6.8 fusion.121
  120.0 8.3 %fusion.119 = (f32[3,512]{1,0:T(4,128)S(1)}, f32[3,512,2048]{2,1,0:T(8,128)}) fusion(pred[512,2048]{1,0:T(8,128)(4,1)S(1)} %broadcast_compare_fusion.4, bf16[2048,3,64]{0,2,1:T(8,128)(2,1)} %get-tuple-element.471, bf16[2048,3,64]{0,2,1:T(8,128)(2,1)} %get-tuple-element.470, s32[]{:T(128)S(6)} %select_n.52), kind=kOutput, calls=%fused_computation.3.clone.1 | convolution fusion | flops 412088832 | bytes 14620676 | tf_op jit(solution)/shard_map/while/body/eval_jaxpr/qhd,khd->hqk/dot_general | solution.py:61
  128.3 6.9 fusion.120
  135.2 6.8 fusion.121
  144.9 8.3 %fusion.119 = (f32[3,512]{1,0:T(4,128)S(1)}, f32[3,512,2048]{2,1,0:T(8,128)}) fusion(pred[512,2048]{1,0:T(8,128)(4,1)S(1)} %broadcast_compare_fusion.4, bf16[2048,3,64]{0,2,1:T(8,128)(2,1)} %get-tuple-element.471, bf16[2048,3,64]{0,2,1:T(8,128)(2,1)} %get-tuple-element.470, s32[]{:T(128)S(6)} %select_n.52), kind=kOutput, calls=%fused_computation.3.clone.1 | convolution fusion | flops 412088832 | bytes 14620676 | tf_op jit(solution)/shard_map/while/body/eval_jaxpr/qhd,khd->hqk/dot_general | solution.py:61
  153.2 6.9 fusion.120
  160.0 6.8 fusion.121
  182.8 15.3 %all_to_all.57 = bf16[4,2,49152]{2,1,0:T(2,128)(2,1)} all-to-all(bf16[4,2,49152]{2,1,0:T(2,128)(2,1)} %reshape.373), channel_id=1, replica_groups=mesh['seq'=4,'dp'=8] {'seq'}, dimensions={0} | all-to-all | bytes 1572864 | tf_op jit(solution)/shard_map/all_to_all | solution.py:164
  237.3 9.3 %all-to-all-done.2 = bf16[512,4,192]{0,2,1:T(8,128)(2,1)} async-done(((bf16[512,4,192]{0,2,1:T(8,128)(2,1)}), bf16[512,4,192]{0,2,1:T(8,128)(2,1)}, u32[]{:S(2)}, u32[]{:S(2)}) %all-to-all-start.2) | async-done | bytes 786464 | tf_op jit(solution)/shard_map/all_to_all | solution.py:197
  252.9 125.6 %while.30 = (s32[]{:T(128)}, f32[2048,3,64]{0,2,1:T(8,128)S(1)}, f32[2048,3,64]{0,2,1:T(8,128)S(1)}, bf16[4,512,3,64]{1,3,2,0:T(8,128)(2,1)}, s32[4]{0:T(128)S(1...) while((s32[]{:T(128)}, f32[2048,3,64]{0,2,1:T(8,128)S(1)}, ...), condition=%wide.region_12.13_spmd.clone, body=%wide.region_10.12_spmd.clone.sunk | while | flops 2047834624 | bytes 185006560 | solution.py:125
  275.1 6.2 fusion.132
  403.5 35.6 %all-to-all-done.3 = bf16[2048,3,1,192]{3,1,2,0:T(4,128)(2,1)} async-done(((bf16[2048,3,1,192]{3,1,2,0:T(4,128)(2,1)}), bf16[2048,3,1,192]{3,1,2,0:T(4,128)(2,1)}, u32[]{:S(2)}, u32[]{:S(2)}) %all-to-all-start.3) | async-done | bytes 2359328 | tf_op jit(solution)/shard_map/all_to_all | solution.py:209
  439.1 6.9 copy.81
  446.0 6.4 reshape.371
  473.3 40.5 %all-reduce = (f32[768]{0:T(1024)}, f32[768]{0:T(1024)}) all-reduce(f32[768]{0:T(1024)S(1)} %get-tuple-element.181, f32[768]{0:T(1024)S(1)} %copy-done.54), channel_id=1, replica_groups=mesh['seq'=4,'dp'=8] {'seq','dp'}, use_global_device_ids=true, to_apply=%region_16.17 | all-reduce | flops 1536 | bytes 12288 | tf_op jit(solution)/shard_map/psum | solution.py:227
  517.0 269.9 %all-reduce.4.cloned.1.call-done = (f32[768,2304]{1,0:T(8,128)}, f32[768,768]{1,0:T(8,128)}, f32[768,2304]{1,0:T(8,128)}, f32[1152,768]{1,0:T(8,128)}) async-done(((f32[768,2304]{1,0:T(8,128)}, f32[768,768]{1,0:T(8,128)}, f32[768,2304]{1,0:T(8,128)}, f32[1152,768]{1,0:T(8,128)}), (f32[768,2304]{1,0:T(8,128)}, f32[768,768]{1,0:T(8,128)}, f32[768,2304]{1,0:T(8,128)}, ...) | async-done | bytes 20054032 | tf_op jit(solution)/shard_map/psum | solution.py:227
  786.9 7.2 copy.118
  (313 shorter events, 266.5 us)
Async XLA Ops:
  7.2 208.6 %copy-start = (bf16[768,2304]{1,0:T(8,128)(2,1)S(1)}, bf16[768,2304]{1,0:T(8,128)(2,1)}, u32[]{:S(2)}) copy-start(bf16[768,2304]{1,0:T(8,128)(2,1)} %param.20) | copy-start | bytes 10616836
  7.2 9.3 %copy-start.52 = (f32[768]{0:T(1024)S(1)}, f32[768]{0:T(1024)}, u32[]{:S(2)}) copy-start(f32[768]{0:T(1024)} %param.16) | copy-start | bytes 9220
  30.1 34.0 %all-to-all-start = ((bf16[512,3,4,192]{0,3,1,2:T(8,128)(2,1)}), bf16[512,3,4,192]{0,3,1,2:T(8,128)(2,1)}, u32[]{:S(2)}, u32[]{:S(2)}) async-start(bf16[512,3,4,192]{0,3,1,2:T(8,128)(2,1)} %pad_maximum_fusion), calls=%async_computation | async-start | bytes 4718592 | tf_op jit(solution)/shard_map/all_to_all | solution.py:158
  78.7 6.9 copy-start.3
  78.7 6.9 copy-start.23
  103.5 6.9 copy-start.3
  103.5 6.9 copy-start.23
  128.3 6.9 copy-start.3
  128.3 6.9 copy-start.23
  153.2 6.9 copy-start.23
  215.4 13.2 %copy-start.5 = (f32[512,768]{1,0:T(8,128)}, f32[512,768]{1,0:T(8,128)S(1)}, u32[]{:S(2)}) copy-start(f32[512,768]{1,0:T(8,128)S(1)} %get-tuple-element.272) | copy-start | bytes 4718596
  215.4 13.2 %copy-start.40 = (f32[512]{0:T(512)}, f32[512]{0:T(512)S(1)}, u32[]{:S(2)}) copy-start(f32[512]{0:T(512)S(1)} %broadcast_multiply_fusion) | copy-start | bytes 6148
  215.7 12.8 %copy-start.42 = (f32[512]{0:T(512)}, f32[512]{0:T(512)S(1)}, u32[]{:S(2)}) copy-start(f32[512]{0:T(512)S(1)} %fusion.65) | copy-start | bytes 6148
  233.1 13.5 %all-to-all-start.2 = ((bf16[512,4,192]{0,2,1:T(8,128)(2,1)}), bf16[512,4,192]{0,2,1:T(8,128)(2,1)}, u32[]{:S(2)}, u32[]{:S(2)}) async-start(bf16[512,4,192]{0,2,1:T(8,128)(2,1)} %bitcast.31), calls=%async_computation.2 | async-start | bytes 1572864 | tf_op jit(solution)/shard_map/all_to_all | solution.py:197
  270.7 10.7 %slice-start = ((s8[6291456]{0:T(1024)(128)(4,1)}), s8[4194304]{0:T(1024)(128)(4,1)S(1)}, s32[]{:S(2)}) async-start(s8[6291456]{0:T(1024)(128)(4,1)} %bitcast.196), calls=%async_computation.5 | async-start | bytes 8388608 | tf_op jit(solution)/shard_map/while
  302.0 10.7 %slice-start = ((s8[6291456]{0:T(1024)(128)(4,1)}), s8[4194304]{0:T(1024)(128)(4,1)S(1)}, s32[]{:S(2)}) async-start(s8[6291456]{0:T(1024)(128)(4,1)} %bitcast.196), calls=%async_computation.5 | async-start | bytes 8388608 | tf_op jit(solution)/shard_map/while
  333.4 10.7 %slice-start = ((s8[6291456]{0:T(1024)(128)(4,1)}), s8[4194304]{0:T(1024)(128)(4,1)S(1)}, s32[]{:S(2)}) async-start(s8[6291456]{0:T(1024)(128)(4,1)} %bitcast.196), calls=%async_computation.5 | async-start | bytes 8388608 | tf_op jit(solution)/shard_map/while
  364.7 10.7 %slice-start = ((s8[6291456]{0:T(1024)(128)(4,1)}), s8[4194304]{0:T(1024)(128)(4,1)S(1)}, s32[]{:S(2)}) async-start(s8[6291456]{0:T(1024)(128)(4,1)} %bitcast.196), calls=%async_computation.5 | async-start | bytes 8388608 | tf_op jit(solution)/shard_map/while
  388.1 51.0 %all-to-all-start.3 = ((bf16[2048,3,1,192]{3,1,2,0:T(4,128)(2,1)}), bf16[2048,3,1,192]{3,1,2,0:T(4,128)(2,1)}, u32[]{:S(2)}, u32[]{:S(2)}) async-start(bf16[2048,3,1,192]{3,1,2,0:T(4,128)(2,1)} %copy.80), calls=%async_computation.3 | async-start | bytes 8388608 | tf_op jit(solution)/shard_map/all_to_all | solution.py:209
  393.1 393.7 %all-reduce.4.cloned.1.call-start = ((), (), s32[]{:S(2)}) async-start(), calls=%async_computation.4 | async-start | bytes 40108032 | tf_op jit(solution)/shard_map/psum | solution.py:227
  471.4 42.4 %copy-start.8 = (f32[512,768]{1,0:T(8,128)S(1)}, f32[512,768]{1,0:T(8,128)}, u32[]{:S(2)}) copy-start(f32[512,768]{1,0:T(8,128)} %copy-done.7) | copy-start | bytes 4718596
  471.4 42.4 %copy-start.49 = (f32[512]{0:T(512)S(1)}, f32[512]{0:T(512)}, u32[]{:S(2)}) copy-start(f32[512]{0:T(512)} %copy-done.48) | copy-start | bytes 6148
  786.9 7.2 copy-start.29
  786.9 8.6 %copy-start.10 = (f32[768,2304]{1,0:T(8,128)S(1)}, f32[768,2304]{1,0:T(8,128)}, u32[]{:S(2)}) copy-start(f32[768,2304]{1,0:T(8,128)} %get-tuple-element.537) | copy-start | bytes 21233668
  (66 other events, 215.3 us)
Sparse Core Ops, SparseCore 0:
  465.2 321.6 all-reduce.3
where the time goes:
time: 816 us; the launch traced here: 809 us
  waiting for transfers between devices  343 us (42%)
  matrix products  188 us (23%)
  local copies, waits for them, and re-layouts  109 us (13%)
  other arithmetic  69.3 us (8%)
  blocking collectives  55.8 us (7%)
  between operations  15.1 us (2%)
  starting transfers between devices  14.6 us (2%)
  loops' own time  13.8 us (2%)
    psum x1, waiting for transfers between devices, on_device(): lax.psum((grad_norm_one, grad_w_qkv, grad_w_out, grad_norm_two, grad_w_in...  270 us
    dot_general x8, matrix products, block_scores(): jnp.einsum('qhd,khd->hqk', query_block, key_heads, preferred_element_type...  53.2 us
    psum x1, blocking collectives, on_device(): lax.psum((grad_norm_one, grad_w_qkv, grad_w_out, grad_norm_two, grad_w_in...  40.5 us
    unnamed x108, local copies, waits for them, and re-layouts  37.3 us
    all_to_all x1, waiting for transfers between devices, on_device(): lax.all_to_all(grad_heads.reshape(row_total, 3, 1, head_width), 'seq', sp...  35.6 us
    all_to_all x1, waiting for transfers between devices, on_device(): lax.all_to_all(outgoing, 'seq', split_axis=2, concat_axis=0, tiled=True)  28.5 us
    reduce_sum x4, other arithmetic, attend_block(): row_sum = jnp.sum(weight, axis=-1, keepdims=True)  27.5 us
    dot_general x4, matrix products, attend_block(): jnp.einsum('hqk,khd->qhd', probs, value_heads, preferred_element_type=jnp...  27 us
  transfers between devices with their start and end apart: 4, of which 4 were waited for; matrix products, arithmetic and copies ran while one was open for 3% of the time, Pallas kernels for 0%

commit v1 on v0

--- a/solution.py
+++ b/solution.py
@@ -11,6 +11,20 @@
 ROTARY_BASE = 160000.0
 SCORE_SCALE = 0.125
 MASKED_SCORE = -1e30
+
+
+def lay_paths(frame, out_dim, local_x):
+    part_next = frame.shape
+    now = frame.reshape(
+        *part_next[:out_dim], local_x, part_next[out_dim] // local_x, *part_next[out_dim + 1 :]
+    )
+    return jnp.moveaxis(now, out_dim, 0)
+
+
+def _start_figure(z, d_out):
+    z = jnp.moveaxis(z, 0, d_out)
+    a_next = z.shape
+    return z.reshape(*a_next[:d_out], a_next[d_out] * a_next[d_out + 1], *a_next[d_out + 2 :])
 
 
 def layer_norm(values, gain_vec):
@@ -206,13 +220,18 @@
         queries, key_heads, value_heads, grad_context, starts, row_max, row_sum, block_rows
     )
     grad_heads = jnp.stack([grad_query, grad_key, grad_value], axis=1).astype(jnp.bfloat16)
-    grad_tok = lax.all_to_all(
-        grad_heads.reshape(row_total, 3, 1, head_width),
-        "seq",
-        split_axis=0,
-        concat_axis=2,
-        tiled=True,
-    )
+
+    def carry_lines(tile_in, mesh_ax, base_x, inner_x):
+        near, moved = (lax.psum(1, axis_name=mesh_ax), lax.axis_index(mesh_ax))
+        small = lay_paths(tile_in, base_x, near)
+        vals = [small[moved]]
+        for pp in [*range(1, near)]:
+            met_up = small[moved ^ pp]
+            vals.append(lax.ppermute(met_up, mesh_ax, [(dd, dd ^ pp) for dd in range(near)]))
+        small = jnp.stack(vals)[moved ^ jnp.arange(near)]
+        return _start_figure(small, inner_x)
+
+    grad_tok = carry_lines(grad_heads.reshape(row_total, 3, 1, head_width), "seq", 0, inner_x=2)
     grad_tok = grad_tok.reshape(shard_len, 3, HEADS, HEAD_DIM)
     grad_projected = unrotate_three(grad_tok.astype(jnp.float32), cosine, sine_table)
     grad_projected = grad_projected.astype(jnp.bfloat16).reshape(shard_len, 3 * D)

time: 816 us -> 775 us (0.950)
  waiting for transfers between devices: 343 us -> 316 us
  local copies, waits for them, and re-layouts: 109 us -> 94.5 us
    all_to_all x1 -> x0, waiting for transfers between devices: 35.6 us -> none  [on_device(): lax.all_to_all(grad_heads.reshape(row_total, 3, 1, head_width), 'seq', sp...]
    ppermute x0 -> x3, waiting for transfers between devices: none -> 15.3 us  [carry_lines(): lax.ppermute(met_up, mesh_ax, [(dd, dd ^ pp) for dd in range(near)])]
    convert_element_type x2 -> x1, local copies, waits for them, and re-layouts: 10.3 us -> 0.51 us  [on_device(): grad_tok.astype(jnp.float32)]
  transfers between devices with their start and end apart: 4 -> 6, of which waited for: 4 -> 5; matrix products, arithmetic and copies ran while one was open for 3% -> 3% of each run, Pallas kernels for 0% -> 0%
where the time goes in v1:
time: 775 us; the launch traced here: 769 us
  waiting for transfers between devices  316 us (41%)
  matrix products  190 us (25%)
  local copies, waits for them, and re-layouts  94.5 us (12%)
  other arithmetic  70.9 us (9%)
  blocking collectives  56.1 us (7%)
  between operations  15.1 us (2%)
  loops' own time  13.6 us (2%)
  starting transfers between devices  13.1 us (2%)
    psum x1, waiting for transfers between devices, on_device(): lax.psum((grad_norm_one, grad_w_qkv, grad_w_out, grad_norm_two, grad_w_in...  268 us
    dot_general x8, matrix products, block_scores(): jnp.einsum('qhd,khd->hqk', query_block, key_heads, preferred_element_type...  53.2 us
    psum x1, blocking collectives, on_device(): lax.psum((grad_norm_one, grad_w_qkv, grad_w_out, grad_norm_two, grad_w_in...  40.7 us
    unnamed x108, local copies, waits for them, and re-layouts  39 us
    all_to_all x1, waiting for transfers between devices, on_device(): lax.all_to_all(outgoing, 'seq', split_axis=2, concat_axis=0, tiled=True)  28.5 us
    reduce_sum x4, other arithmetic, attend_block(): row_sum = jnp.sum(weight, axis=-1, keepdims=True)  27.5 us
    dot_general x4, matrix products, attend_block(): jnp.einsum('hqk,khd->qhd', probs, value_heads, preferred_element_type=jnp...  27 us
    dot_general x4, matrix products, back_block(): jnp.einsum('hqk,qhd->khd', probs_low, grad_block, preferred_element_type=...  24.9 us
  transfers between devices with their start and end apart: 6, of which 5 were waited for; matrix products, arithmetic and copies ran while one was open for 3% of the time, Pallas kernels for 0%

profile of v1, /device:TPU:0, one launch (start us, length us, event | category | flops | bytes accessed | tf_op | source)
XLA Modules:
  0.0 769.0 jit_solution(16149336112347676856)
XLA Ops:
  35.5 28.5 %all-to-all-done = bf16[512,3,4,192]{0,3,1,2:T(8,128)(2,1)} async-done(((bf16[512,3,4,192]{0,3,1,2:T(8,128)(2,1)}), bf16[512,3,4,192]{0,3,1,2:T(8,128)(2,1)}, u32[]{:S(2)}, u32[]{:S(2)}) %all-to-all-start) | async-done | bytes 2359328 | tf_op jit(solution)/shard_map/all_to_all | solution.py:172
  68.4 99.3 %while.29 = (s32[]{:T(128)}, bf16[4,512,3,64]{1,3,2,0:T(8,128)(2,1)}, f32[4,3,512,1]{2,1,3,0:T(4,128)}, f32[4,3,512,1]{2,1,3,0:T(4,128)}, s32[4]{0:T(128)S(1)}, ...) while((s32[]{:T(128)}, ...), condition=%wide.region_5.6_spmd, body=%wide.region_2.5_spmd.sunk | while | flops 844100608 | bytes 53621036 | solution.py:97
  70.4 8.3 %fusion.120 = (f32[3,512]{1,0:T(4,128)S(1)}, f32[3,512,2048]{2,1,0:T(8,128)}) fusion(pred[512,2048]{1,0:T(8,128)(4,1)S(1)} %broadcast_compare_fusion.4, bf16[2048,3,64]{0,2,1:T(8,128)(2,1)} %get-tuple-element.475, bf16[2048,3,64]{0,2,1:T(8,128)(2,1)} %get-tuple-element.474, s32[]{:T(128)S(6)} %select_n.82), kind=kOutput, calls=%fused_computation.4.clone.1 | convolution fusion | flops 412088832 | bytes 14620676 | tf_op jit(solution)/shard_map/while/body/eval_jaxpr/qhd,khd->hqk/dot_general | solution.py:75
  78.7 6.9 fusion.121
  85.6 6.8 fusion.122
  95.2 8.3 %fusion.120 = (f32[3,512]{1,0:T(4,128)S(1)}, f32[3,512,2048]{2,1,0:T(8,128)}) fusion(pred[512,2048]{1,0:T(8,128)(4,1)S(1)} %broadcast_compare_fusion.4, bf16[2048,3,64]{0,2,1:T(8,128)(2,1)} %get-tuple-element.475, bf16[2048,3,64]{0,2,1:T(8,128)(2,1)} %get-tuple-element.474, s32[]{:T(128)S(6)} %select_n.82), kind=kOutput, calls=%fused_computation.4.clone.1 | convolution fusion | flops 412088832 | bytes 14620676 | tf_op jit(solution)/shard_map/while/body/eval_jaxpr/qhd,khd->hqk/dot_general | solution.py:75
  103.5 6.9 fusion.121
  110.4 6.8 fusion.122
  120.0 8.3 %fusion.120 = (f32[3,512]{1,0:T(4,128)S(1)}, f32[3,512,2048]{2,1,0:T(8,128)}) fusion(pred[512,2048]{1,0:T(8,128)(4,1)S(1)} %broadcast_compare_fusion.4, bf16[2048,3,64]{0,2,1:T(8,128)(2,1)} %get-tuple-element.475, bf16[2048,3,64]{0,2,1:T(8,128)(2,1)} %get-tuple-element.474, s32[]{:T(128)S(6)} %select_n.82), kind=kOutput, calls=%fused_computation.4.clone.1 | convolution fusion | flops 412088832 | bytes 14620676 | tf_op jit(solution)/shard_map/while/body/eval_jaxpr/qhd,khd->hqk/dot_general | solution.py:75
  128.3 6.9 fusion.121
  135.2 6.8 fusion.122
  144.9 8.3 %fusion.120 = (f32[3,512]{1,0:T(4,128)S(1)}, f32[3,512,2048]{2,1,0:T(8,128)}) fusion(pred[512,2048]{1,0:T(8,128)(4,1)S(1)} %broadcast_compare_fusion.4, bf16[2048,3,64]{0,2,1:T(8,128)(2,1)} %get-tuple-element.475, bf16[2048,3,64]{0,2,1:T(8,128)(2,1)} %get-tuple-element.474, s32[]{:T(128)S(6)} %select_n.82), kind=kOutput, calls=%fused_computation.4.clone.1 | convolution fusion | flops 412088832 | bytes 14620676 | tf_op jit(solution)/shard_map/while/body/eval_jaxpr/qhd,khd->hqk/dot_general | solution.py:75
  153.2 6.9 fusion.121
  160.1 6.8 fusion.122
  182.8 15.3 %all_to_all.48 = bf16[4,2,49152]{2,1,0:T(2,128)(2,1)} all-to-all(bf16[4,2,49152]{2,1,0:T(2,128)(2,1)} %reshape.394), channel_id=1, replica_groups=mesh['seq'=4,'dp'=8] {'seq'}, dimensions={0} | all-to-all | bytes 1572864 | tf_op jit(solution)/shard_map/all_to_all | solution.py:178
  253.1 125.4 %while.30 = (s32[]{:T(128)}, f32[2048,3,64]{0,2,1:T(8,128)S(1)}, f32[2048,3,64]{0,2,1:T(8,128)S(1)}, bf16[4,512,3,64]{1,3,2,0:T(8,128)(2,1)}, s32[4]{0:T(128)S(1...) while((s32[]{:T(128)}, f32[2048,3,64]{0,2,1:T(8,128)S(1)}, ...), condition=%wide.region_12.13_spmd.clone, body=%wide.region_10.12_spmd.clone.sunk | while | flops 2047834624 | bytes 185006560 | solution.py:139
  275.2 6.2 fusion.133
  306.6 6.2 fusion.133
  338.0 6.2 fusion.133
  395.7 6.3 collective-permute-done.2
  402.0 8.9 %collective-permute-done.1 = bf16[512,3,1,192]{0,3,1,2:T(8,128)(2,1)S(1)} collective-permute-done((bf16[512,3,1,192]{0,3,1,2:T(8,128)(2,1)S(1)}, bf16[512,3,1,192]{0,3,1,2:T(8,128)(2,1)S(1)}, u32[]{:S(2)}, u32[]{:S(2)}) %collective-permute-start.1) | collective-permute-done | bytes 589856 | tf_op jit(solution)/shard_map/ppermute | solution.py:230
  434.9 40.7 %all-reduce = (f32[768]{0:T(1024)}, f32[768]{0:T(1024)}) all-reduce(f32[768]{0:T(1024)S(1)} %get-tuple-element.181, f32[768]{0:T(1024)S(1)} %copy-done.54), channel_id=1, replica_groups=mesh['seq'=4,'dp'=8] {'seq','dp'}, use_global_device_ids=true, to_apply=%region_16.17 | all-reduce | flops 1536 | bytes 12288 | tf_op jit(solution)/shard_map/psum | solution.py:246
  478.9 268.0 %all-reduce.4.cloned.1.call-done = (f32[768,2304]{1,0:T(8,128)}, f32[768,768]{1,0:T(8,128)}, f32[768,2304]{1,0:T(8,128)}, f32[1152,768]{1,0:T(8,128)}) async-done(((f32[768,2304]{1,0:T(8,128)}, f32[768,768]{1,0:T(8,128)}, f32[768,2304]{1,0:T(8,128)}, f32[1152,768]{1,0:T(8,128)}), (f32[768,2304]{1,0:T(8,128)}, f32[768,768]{1,0:T(8,128)}, f32[768,2304]{1,0:T(8,128)}, ...) | async-done | bytes 20054032 | tf_op jit(solution)/shard_map/psum | solution.py:246
  746.9 7.2 copy.89
  (322 shorter events, 258.7 us)
Async XLA Ops:
  7.2 208.5 %copy-start = (bf16[768,2304]{1,0:T(8,128)(2,1)S(1)}, bf16[768,2304]{1,0:T(8,128)(2,1)}, u32[]{:S(2)}) copy-start(bf16[768,2304]{1,0:T(8,128)(2,1)} %param.20) | copy-start | bytes 10616836
  7.2 9.3 %copy-start.52 = (f32[768]{0:T(1024)S(1)}, f32[768]{0:T(1024)}, u32[]{:S(2)}) copy-start(f32[768]{0:T(1024)} %param.16) | copy-start | bytes 9220
  30.1 33.9 %all-to-all-start = ((bf16[512,3,4,192]{0,3,1,2:T(8,128)(2,1)}), bf16[512,3,4,192]{0,3,1,2:T(8,128)(2,1)}, u32[]{:S(2)}, u32[]{:S(2)}) async-start(bf16[512,3,4,192]{0,3,1,2:T(8,128)(2,1)} %pad_maximum_fusion), calls=%async_computation | async-start | bytes 4718592 | tf_op jit(solution)/shard_map/all_to_all | solution.py:172
  78.7 6.9 copy-start.23
  103.5 6.9 copy-start.23
  128.3 6.9 copy-start.23
  153.2 6.9 copy-start.23
  215.3 13.2 %copy-start.5 = (f32[512,768]{1,0:T(8,128)}, f32[512,768]{1,0:T(8,128)S(1)}, u32[]{:S(2)}) copy-start(f32[512,768]{1,0:T(8,128)S(1)} %get-tuple-element.276) | copy-start | bytes 4718596
  215.3 13.2 %copy-start.40 = (f32[512]{0:T(512)}, f32[512]{0:T(512)S(1)}, u32[]{:S(2)}) copy-start(f32[512]{0:T(512)S(1)} %broadcast_multiply_fusion) | copy-start | bytes 6148
  215.7 12.8 %copy-start.42 = (f32[512]{0:T(512)}, f32[512]{0:T(512)S(1)}, u32[]{:S(2)}) copy-start(f32[512]{0:T(512)S(1)} %fusion.65) | copy-start | bytes 6148
  233.0 13.5 %all-to-all-start.2 = ((bf16[512,4,192]{0,2,1:T(8,128)(2,1)}), bf16[512,4,192]{0,2,1:T(8,128)(2,1)}, u32[]{:S(2)}, u32[]{:S(2)}) async-start(bf16[512,4,192]{0,2,1:T(8,128)(2,1)} %bitcast.31), calls=%async_computation.2 | async-start | bytes 1572864 | tf_op jit(solution)/shard_map/all_to_all | solution.py:211
  237.2 509.7 %all-reduce.4.cloned.1.call-start = ((), (), s32[]{:S(2)}) async-start(), calls=%async_computation.3 | async-start | bytes 40108032 | tf_op jit(solution)/shard_map/psum | solution.py:246
  270.8 10.7 %slice-start = ((s8[6291456]{0:T(1024)(128)(4,1)}), s8[4194304]{0:T(1024)(128)(4,1)S(1)}, s32[]{:S(2)}) async-start(s8[6291456]{0:T(1024)(128)(4,1)} %bitcast.210), calls=%async_computation.4 | async-start | bytes 8388608 | tf_op jit(solution)/shard_map/while
  302.2 10.7 %slice-start = ((s8[6291456]{0:T(1024)(128)(4,1)}), s8[4194304]{0:T(1024)(128)(4,1)S(1)}, s32[]{:S(2)}) async-start(s8[6291456]{0:T(1024)(128)(4,1)} %bitcast.210), calls=%async_computation.4 | async-start | bytes 8388608 | tf_op jit(solution)/shard_map/while
  333.5 10.7 %slice-start = ((s8[6291456]{0:T(1024)(128)(4,1)}), s8[4194304]{0:T(1024)(128)(4,1)S(1)}, s32[]{:S(2)}) async-start(s8[6291456]{0:T(1024)(128)(4,1)} %bitcast.210), calls=%async_computation.4 | async-start | bytes 8388608 | tf_op jit(solution)/shard_map/while
  364.9 10.7 %slice-start = ((s8[6291456]{0:T(1024)(128)(4,1)}), s8[4194304]{0:T(1024)(128)(4,1)S(1)}, s32[]{:S(2)}) async-start(s8[6291456]{0:T(1024)(128)(4,1)} %bitcast.210), calls=%async_computation.4 | async-start | bytes 8388608 | tf_op jit(solution)/shard_map/while
  384.8 17.2 %collective-permute-start.2 = (bf16[512,3,1,192]{0,3,1,2:T(8,128)(2,1)S(1)}, bf16[512,3,1,192]{0,3,1,2:T(8,128)(2,1)S(1)}, u32[]{:S(2)}, u32[]{:S(2)}) collective-permute-start(bf16[512,3,1,192]{0,3,1,2:T(8,128)(2,1)S(1)} %get-tuple-element.254), channel_id=1, source_target_pairs={{0,24},{8,16},{16,8},{24,0},{1,25},{9,17},{17,9},{25,1},{2,26},{10... | collective-permute-start | bytes 1769480 | tf_op jit(solution)/shard_map/ppermute | solution.py:230
  386.3 24.7 %collective-permute-start.1 = (bf16[512,3,1,192]{0,3,1,2:T(8,128)(2,1)S(1)}, bf16[512,3,1,192]{0,3,1,2:T(8,128)(2,1)S(1)}, u32[]{:S(2)}, u32[]{:S(2)}) collective-permute-start(bf16[512,3,1,192]{0,3,1,2:T(8,128)(2,1)S(1)} %get-tuple-element.255), channel_id=1, source_target_pairs={{0,16},{8,24},{16,0},{24,8},{1,17},{9,25},{17,1},{25,9},{2,18},{10... | collective-permute-start | bytes 1769480 | tf_op jit(solution)/shard_map/ppermute | solution.py:230
  387.7 23.2 %collective-permute-start = (bf16[512,3,1,192]{0,3,1,2:T(8,128)(2,1)S(1)}, bf16[512,3,1,192]{0,3,1,2:T(8,128)(2,1)S(1)}, u32[]{:S(2)}, u32[]{:S(2)}) collective-permute-start(bf16[512,3,1,192]{0,3,1,2:T(8,128)(2,1)S(1)} %get-tuple-element.256), channel_id=1, source_target_pairs={{0,8},{8,0},{16,24},{24,16},{1,9},{9,1},{17,25},{25,17},{2,10},{10... | collective-permute-start | bytes 1769480 | tf_op jit(solution)/shard_map/ppermute | solution.py:230
  433.0 42.7 %copy-start.9 = (f32[512,768]{1,0:T(8,128)S(1)}, f32[512,768]{1,0:T(8,128)}, u32[]{:S(2)}) copy-start(f32[512,768]{1,0:T(8,128)} %copy-done.8) | copy-start | bytes 4718596
  433.0 42.6 %copy-start.13 = (bf16[1,512,768]{2,1,0:T(8,128)(2,1)S(1)}, bf16[1,512,768]{2,1,0:T(8,128)(2,1)}, u32[]{:S(2)}) copy-start(bf16[1,512,768]{2,1,0:T(8,128)(2,1)} %param.15) | copy-start | bytes 2359300
  433.0 42.6 %copy-start.49 = (f32[512]{0:T(512)S(1)}, f32[512]{0:T(512)}, u32[]{:S(2)}) copy-start(f32[512]{0:T(512)} %copy-done.48) | copy-start | bytes 6148
  746.9 7.2 copy-start.29
  746.9 8.6 %copy-start.11 = (f32[768,2304]{1,0:T(8,128)S(1)}, f32[768,2304]{1,0:T(8,128)}, u32[]{:S(2)}) copy-start(f32[768,2304]{1,0:T(8,128)} %get-tuple-element.541) | copy-start | bytes 21233668
  (68 other events, 247.5 us)
Sparse Core Ops, SparseCore 0:
  425.1 321.7 all-reduce.3
